TPU v7x, 128 devices: a whole 4x4x4 slice. The times are simulated.
128 devices in a mesh: shard: 16 (over z, x), tensor: 8 (over y, core).
Axes of the slice: x: 4, y: 4, z: 4, core: 2. Of those that a mesh axis runs over, the one named last changes fastest.
Arguments:
- gradient: bfloat16 [768, 3072], P('shard', 'tensor'), may hold values from -12 to 12
- moment_one: float32 [768, 3072], P('shard', 'tensor'), may hold values from -6 to 6
- moment_two: float32 [768, 3072], P('shard', 'tensor'), may hold values from 0.5 to 8
- stat_left: float32 [768, 768], P('shard'), may hold values from -1 to 3, as said below
- stat_right: float32 [3072, 3072], P('shard', 'tensor'), may hold values from -1 to 3, as said below
- basis_left: float32 [768, 768], P('shard'), may hold values from -3 to 25, as said below
- basis_right: float32 [3072, 3072], P('shard', 'tensor'), may hold values from -3 to 47, as said below
Outputs:
- update: bfloat16 [768, 3072], P('shard', 'tensor')
- new_moment_one: float32 [768, 3072], P('shard', 'tensor')
- new_moment_two: float32 [768, 3072], P('shard', 'tensor')
- new_stat_left: float32 [768, 768], P('shard')
- new_stat_right: float32 [3072, 3072], P('shard', 'tensor')
- new_basis_left: float32 [768, 768], P('shard')
- new_basis_right: float32 [3072, 3072], P('shard', 'tensor')
Inputs may be any that keep to these rules, and one draw needn't show every extreme that they name: `stat_left`: symmetric and positive definite. `stat_right`: symmetric and positive definite. `basis_left`: full rank. `basis_right`: full rank.
All inputs are finite; a program needn't handle non-finite values.
Results may differ from a plain program's by a relative error of at most 0.011.
Values may be sent and summed in bfloat16 or wider, within the bound.
A program may use at most 64 MiB of HBM per device.

v0:
```python
import math
import jax
import jax.numpy as jnp
from jax import lax
from jax.sharding import PartitionSpec as P

D = 768
FF = 3072
NS_STEPS = 2
beta_one = 0.95
beta_two = 0.95
beta_stat = 0.95
correction = 1.0 - 0.95**10
adam_eps = 1e-08
highest = lax.Precision.HIGHEST


def blend_stat(previous, product, divisor):
    return beta_stat * previous + (1.0 - beta_stat) * (product / divisor)


def adam_moments(rotated, moment_one, moment_two):
    first_moment = beta_one * moment_one + (1.0 - beta_one) * rotated
    second_moment = beta_two * moment_two + (1.0 - beta_two) * (rotated * rotated)
    direction = (
        first_moment / correction / (jnp.sqrt(second_moment / correction) + adam_eps)
    ).astype(jnp.bfloat16)
    return (first_moment, second_moment, direction)


def local(gradient, moment_one, moment_two, stat_left, stat_right, basis_left, basis_right):
    rows_left = gradient.shape[0]
    rows_right = stat_right.shape[0]
    cols_right = stat_right.shape[1]
    shard_pos = lax.axis_index("shard")
    tensor_pos = lax.axis_index("tensor")
    row_start = shard_pos * rows_left
    grad_cols = lax.all_gather(gradient, "shard", axis=0, tiled=True)
    left_terms = jnp.dot(gradient, grad_cols.T, preferred_element_type=jnp.float32)
    gram_rows = lax.psum(left_terms.astype(jnp.bfloat16), "tensor").astype(jnp.float32)
    new_stat_left = blend_stat(stat_left, gram_rows, FF)
    grad_rows = lax.all_gather(gradient, "tensor", axis=1, tiled=True)
    gram_block = lax.psum_scatter(
        jnp.dot(grad_rows.T, gradient, preferred_element_type=jnp.float32).astype(jnp.bfloat16),
        "shard",
        scatter_dimension=0,
        tiled=True,
    ).astype(jnp.float32)
    new_stat_right = blend_stat(stat_right, gram_block, D)
    basis_all = lax.all_gather(basis_left, "shard", axis=0, tiled=True)
    left_q_all = basis_all / math.sqrt(D)
    left_qb_all = left_q_all.astype(jnp.bfloat16)
    left_qb_own = lax.dynamic_slice_in_dim(left_qb_all, row_start, rows_left, 0)
    left_cols_own = lax.dynamic_slice_in_dim(left_qb_all, row_start, rows_left, 1)
    half_rotated = jnp.dot(left_cols_own.T, grad_cols, preferred_element_type=jnp.float32).astype(
        jnp.bfloat16
    )
    right_q = basis_right / math.sqrt(FF)
    right_qb = right_q.astype(jnp.bfloat16)
    right_cols_b = lax.all_gather(right_qb, "shard", axis=0, tiled=True)
    half_full = lax.all_gather(half_rotated, "tensor", axis=1, tiled=True)
    rotated = jnp.dot(half_full, right_cols_b, preferred_element_type=jnp.float32)
    new_moment_one, new_moment_two, direction = adam_moments(rotated, moment_one, moment_two)
    back_half = jnp.dot(
        left_qb_own,
        lax.all_gather(direction, "shard", axis=0, tiled=True),
        preferred_element_type=jnp.float32,
    ).astype(jnp.bfloat16)
    back_terms = jnp.dot(back_half, right_cols_b.T, preferred_element_type=jnp.float32)
    update = lax.psum_scatter(back_terms, "tensor", scatter_dimension=1, tiled=True).astype(
        jnp.bfloat16
    )
    stat_rows = lax.all_gather(new_stat_right, "tensor", axis=1, tiled=True)
    power_right = jnp.dot(
        stat_rows,
        lax.all_gather(right_q, "shard", axis=0, tiled=True),
        precision=highest,
        preferred_element_type=jnp.float32,
    )
    power_left = jnp.dot(
        new_stat_left, left_q_all, precision=highest, preferred_element_type=jnp.float32
    )
    local_left = jnp.sum(power_left * power_left)
    local_right = jnp.sum(power_right * power_right)
    total_left = lax.psum(local_left, "shard")
    total_right = lax.psum(local_right, ("shard", "tensor"))
    iterate_left = power_left * (math.sqrt(D) / (4.0 * jnp.sqrt(total_left)))
    for iteration in range(NS_STEPS):
        partial_gram = jnp.dot(
            iterate_left.T, iterate_left, precision=highest, preferred_element_type=jnp.float32
        )
        gram_left = lax.psum(partial_gram.astype(jnp.bfloat16), "shard").astype(jnp.float32)
        iterate_left = 1.5 * iterate_left - 0.5 * jnp.dot(
            iterate_left, gram_left, precision=highest, preferred_element_type=jnp.float32
        )
    iterate_right = power_right * (math.sqrt(FF) / (4.0 * jnp.sqrt(total_right)))
    row_ids = shard_pos * rows_right + lax.broadcasted_iota(jnp.int32, (rows_right, cols_right), 0)
    col_ids = tensor_pos * cols_right + lax.broadcasted_iota(jnp.int32, (rows_right, cols_right), 1)
    identity_tile = (row_ids == col_ids).astype(jnp.float32)
    for iteration in range(NS_STEPS):
        rounded_iterate = iterate_right.astype(jnp.bfloat16)
        iterate_rows = lax.all_gather(rounded_iterate, "tensor", axis=1, tiled=True)
        gram_right = lax.psum_scatter(
            jnp.dot(iterate_rows.T, rounded_iterate, preferred_element_type=jnp.float32).astype(
                jnp.bfloat16
            ),
            "shard",
            scatter_dimension=0,
            tiled=True,
        ).astype(jnp.float32)
        mixing = (1.5 * identity_tile - 0.5 * gram_right).astype(jnp.bfloat16)
        iterate_right = jnp.dot(
            iterate_rows,
            lax.all_gather(mixing, "shard", axis=0, tiled=True),
            preferred_element_type=jnp.float32,
        )
    return (
        update,
        new_moment_one,
        new_moment_two,
        new_stat_left,
        new_stat_right,
        iterate_left * math.sqrt(D),
        iterate_right * math.sqrt(FF),
    )


def solution(mesh):
    placed = (
        P("shard", "tensor"),
        P("shard", "tensor"),
        P("shard", "tensor"),
        P("shard", None),
        P("shard", "tensor"),
        P("shard", None),
        P("shard", "tensor"),
    )
    return jax.shard_map(
        local,
        mesh=mesh,
        in_specs=placed,
        out_specs=(
            P("shard", "tensor"),
            P("shard", "tensor"),
            P("shard", "tensor"),
            P("shard", None),
            P("shard", "tensor"),
            P("shard", None),
            P("shard", "tensor"),
        ),
        check_vma=False,
    )
```

profile of v0, /device:TPU:0, one launch (start us, length us, event | category | flops | bytes accessed | tf_op | source)
XLA Modules:
  0.0 935.4 jit_solution(6653130991982937467)
XLA Ops:
  7.2 13.8 %all_gather.41 = bf16[48,3072]{1,0:T(8,128)(2,1)S(1)} all-gather(bf16[48,384]{1,0:T(8,128)(2,1)} %param.7), channel_id=1, replica_groups=mesh['shard'=16,'tensor'=8] {'tensor'}, dimensions={1}, use_global_device_ids=true | all-gather | bytes 331776 | tf_op jit(solution)/shard_map/all_gather | solution.py:42
  24.1 77.6 %reduce-scatter.7.cloned.1.call-done = bf16[192,384]{1,0:T(8,128)(2,1)} async-done(((bf16[3072,384]{1,0:T(8,128)(2,1)}), bf16[192,384]{1,0:T(8,128)(2,1)}) %reduce-scatter.7.cloned.1.call-update) | async-done | bytes 147472 | tf_op jit(solution)/shard_map/reduce_scatter | solution.py:43
  104.4 24.5 %all-gather.13.cloned.1.call-done = f32[192,3072]{1,0:T(8,128)} async-done(((f32[192,384]{1,0:T(8,128)}), f32[192,3072]{1,0:T(8,128)}) %all-gather.13.cloned.1.call-update) | async-done | bytes 2359312 | tf_op jit(solution)/shard_map/all_gather | solution.py:73
  128.9 57.2 %all-gather.15.cloned.1.call-done = f32[3072,384]{1,0:T(8,128)} async-done(((f32[192,384]{1,0:T(8,128)}), f32[3072,384]{1,0:T(8,128)}) %all-gather.15.cloned.1.call-update) | async-done | bytes 4718608 | tf_op jit(solution)/shard_map/all_gather | solution.py:76
  186.1 7.8 multiply_reduce_fusion
  193.9 64.5 %psum.39 = f32[]{:T(128)} all-reduce(f32[]{:T(128)} %get-tuple-element.14), channel_id=1, replica_groups=mesh['shard'=16,'tensor'=8] {'shard','tensor'}, use_global_device_ids=true, to_apply=%region_8.0 | all-reduce | flops 1 | bytes 8 | tf_op jit(solution)/shard_map/psum | solution.py:86
  259.9 21.0 %all-gather.17.cloned.1.call-done = bf16[192,3072]{1,0:T(8,128)(2,1)} async-done(((bf16[192,384]{1,0:T(8,128)(2,1)}), bf16[192,3072]{1,0:T(8,128)(2,1)}) %all-gather.17.cloned.1.call-update) | async-done | bytes 1179664 | tf_op jit(solution)/shard_map/all_gather | solution.py:102
  280.9 3.7 convolution_convert_fusion.1
  284.7 75.9 %reduce-scatter.9.cloned.1.call-done = bf16[192,384]{1,0:T(8,128)(2,1)} async-done(((bf16[3072,384]{1,0:T(8,128)(2,1)}), bf16[192,384]{1,0:T(8,128)(2,1)}) %reduce-scatter.9.cloned.1.call-update) | async-done | bytes 147472 | tf_op jit(solution)/shard_map/reduce_scatter | solution.py:103
  362.3 23.6 %all_gather.37 = bf16[768,384]{1,0:T(8,128)(2,1)S(1)} all-gather(bf16[48,384]{1,0:T(8,128)(2,1)S(1)} %copy-done.7), channel_id=1, replica_groups=mesh['shard'=16,'tensor'=8] {'shard'}, dimensions={0}, use_global_device_ids=true | all-gather | bytes 626688 | tf_op jit(solution)/shard_map/all_gather | solution.py:38
  387.7 21.1 %all-gather.19.cloned.1.call-done = bf16[3072,384]{1,0:T(8,128)(2,1)} async-done(((bf16[192,384]{1,0:T(8,128)(2,1)}), bf16[3072,384]{1,0:T(8,128)(2,1)}) %all-gather.19.cloned.1.call-update) | async-done | bytes 2359312 | tf_op jit(solution)/shard_map/all_gather | solution.py:114
  412.5 53.3 %all-reduce.4.cloned.1.call-done = bf16[48,768]{1,0:T(8,128)(2,1)} async-done(((bf16[48,768]{1,0:T(8,128)(2,1)}), bf16[48,768]{1,0:T(8,128)(2,1)}) %all-reduce.4.cloned.1.call-update) | async-done | bytes 73744 | tf_op jit(solution)/shard_map/psum | solution.py:40
  466.8 47.2 %all-gather.9.cloned.1.call-done = f32[768,768]{1,0:T(8,128)} async-done(((f32[48,768]{1,0:T(8,128)}), f32[768,768]{1,0:T(8,128)}) %all-gather.9.cloned.1.call-update) | async-done | bytes 2359312 | tf_op jit(solution)/shard_map/all_gather | solution.py:50
  513.9 3.8 multiply_reduce_fusion.1
  517.7 39.0 %psum.36 = f32[]{:T(128)} all-reduce(f32[]{:T(128)} %get-tuple-element.12), channel_id=1, replica_groups=mesh['shard'=16,'tensor'=8] {'shard'}, use_global_device_ids=true, to_apply=%region_4.0 | all-reduce | flops 1 | bytes 8 | tf_op jit(solution)/shard_map/psum | solution.py:85
  560.7 3.9 convolution_convert_fusion
  565.9 13.2 %all_gather.38 = bf16[48,3072]{1,0:T(8,128)(2,1)S(1)} all-gather(bf16[48,384]{1,0:T(8,128)(2,1)S(1)} %convolution_convert_fusion.8), channel_id=1, replica_groups=mesh['shard'=16,'tensor'=8] {'tensor'}, dimensions={1}, use_global_device_ids=true | all-gather | bytes 331776 | tf_op jit(solution)/shard_map/all_gather | solution.py:61
  579.2 8.1 all-gather.11.cloned.1.call-done
  590.2 24.4 %all_gather.40 = bf16[768,384]{1,0:T(8,128)(2,1)S(1)} all-gather(bf16[48,384]{1,0:T(8,128)(2,1)S(1)} %get-tuple-element.7), channel_id=1, replica_groups=mesh['shard'=16,'tensor'=8] {'shard'}, dimensions={0}, use_global_device_ids=true | all-gather | bytes 626688 | tf_op jit(solution)/shard_map/all_gather | solution.py:66
  617.4 60.1 %all-reduce.6.cloned.1.call-done = bf16[768,768]{1,0:T(8,128)(2,1)} async-done(((bf16[768,768]{1,0:T(8,128)(2,1)}), bf16[768,768]{1,0:T(8,128)(2,1)}) %all-reduce.6.cloned.1.call-update) | async-done | bytes 1179664 | tf_op jit(solution)/shard_map/psum | solution.py:92
  682.6 73.2 %reduce-scatter.11.cloned.1.call-done = bf16[192,384]{1,0:T(8,128)(2,1)} async-done(((bf16[3072,384]{1,0:T(8,128)(2,1)}), bf16[192,384]{1,0:T(8,128)(2,1)}) %reduce-scatter.11.cloned.1.call-update) | async-done | bytes 147472 | tf_op jit(solution)/shard_map/reduce_scatter | solution.py:103
  757.5 31.4 %reduce-scatter.5.cloned.1.call-done = f32[48,384]{1,0:T(8,128)} async-done(((f32[48,3072]{1,0:T(8,128)}), f32[48,384]{1,0:T(8,128)}) %reduce-scatter.5.cloned.1.call-update) | async-done | bytes 73744 | tf_op jit(solution)/shard_map/reduce_scatter | solution.py:70
  790.5 87.6 %all-reduce.8.cloned.1.call-done = bf16[768,768]{1,0:T(8,128)(2,1)} async-done(((bf16[768,768]{1,0:T(8,128)(2,1)}), bf16[768,768]{1,0:T(8,128)(2,1)}) %all-reduce.8.cloned.1.call-update) | async-done | bytes 1179664 | tf_op jit(solution)/shard_map/psum | solution.py:92
  880.7 45.0 %all-gather.23.cloned.1.call-done = bf16[3072,384]{1,0:T(8,128)(2,1)} async-done(((bf16[192,384]{1,0:T(8,128)(2,1)}), bf16[3072,384]{1,0:T(8,128)(2,1)}) %all-gather.23.cloned.1.call-update) | async-done | bytes 2359312 | tf_op jit(solution)/shard_map/all_gather | solution.py:114
  (78 shorter events, 39.0 us)
Async XLA Ops:
  7.2 94.6 %reduce-scatter.7.cloned.1.call-start = ((), (), s32[]{:S(2)}) async-start(), calls=%async_computation.8 | async-start | bytes 2506752 | tf_op jit(solution)/shard_map/reduce_scatter | solution.py:43
  21.0 80.8 %copy-start.8 = (f32[192,384]{1,0:T(8,128)S(1)}, f32[192,384]{1,0:T(8,128)}, u32[]{:S(2)}) copy-start(f32[192,384]{1,0:T(8,128)} %param.11) | copy-start | bytes 884740
  24.1 79.5 %copy-start.9 = (f32[192,384]{1,0:T(8,128)S(1)}, f32[192,384]{1,0:T(8,128)}, u32[]{:S(2)}) copy-start(f32[192,384]{1,0:T(8,128)} %param.13) | copy-start | bytes 884740
  24.1 104.8 %all-gather.13.cloned.1.call-start = ((), (), s32[]{:S(2)}) async-start(), calls=%async_computation.11 | async-start | bytes 2654208 | tf_op jit(solution)/shard_map/all_gather | solution.py:73
  103.5 82.6 %all-gather.15.cloned.1.call-start = ((), (), s32[]{:S(2)}) async-start(), calls=%async_computation.12 | async-start | bytes 5013504 | tf_op jit(solution)/shard_map/all_gather | solution.py:76
  104.4 176.5 %all-gather.17.cloned.1.call-start = ((), (), s32[]{:S(2)}) async-start(), calls=%async_computation.13 | async-start | bytes 1327104 | tf_op jit(solution)/shard_map/all_gather | solution.py:102
  259.8 102.5 %copy-start.7 = (bf16[48,384]{1,0:T(8,128)(2,1)S(1)}, bf16[48,384]{1,0:T(8,128)(2,1)}, u32[]{:S(2)}) copy-start(bf16[48,384]{1,0:T(8,128)(2,1)} %param.7) | copy-start | bytes 110596
  259.8 100.7 %reduce-scatter.9.cloned.1.call-start = ((), (), s32[]{:S(2)}) async-start(), calls=%async_computation.14 | async-start | bytes 2506752 | tf_op jit(solution)/shard_map/reduce_scatter | solution.py:103
  284.6 124.2 %copy-start.4 = (bf16[192,3072]{1,0:T(8,128)(2,1)S(1)}, bf16[192,3072]{1,0:T(8,128)(2,1)}, u32[]{:S(2)}) copy-start(bf16[192,3072]{1,0:T(8,128)(2,1)} %all-gather.17.cloned.1.call-done) | copy-start | bytes 3538948
  284.6 124.1 %all-gather.19.cloned.1.call-start = ((), (), s32[]{:S(2)}) async-start(), calls=%async_computation.15 | async-start | bytes 2506752 | tf_op jit(solution)/shard_map/all_gather | solution.py:114
  362.3 103.5 %all-reduce.4.cloned.1.call-start = ((), (), s32[]{:S(2)}) async-start(), calls=%async_computation.7 | async-start | bytes 147456 | tf_op jit(solution)/shard_map/psum | solution.py:40
  386.9 127.0 %all-gather.9.cloned.1.call-start = ((), (), s32[]{:S(2)}) async-start(), calls=%async_computation.4 | async-start | bytes 2506752 | tf_op jit(solution)/shard_map/all_gather | solution.py:50
  387.6 78.2 %copy-start.10 = (f32[48,768]{1,0:T(8,128)S(1)}, f32[48,768]{1,0:T(8,128)}, u32[]{:S(2)}) copy-start(f32[48,768]{1,0:T(8,128)} %param.10) | copy-start | bytes 442372
  387.6 173.0 %all-gather.21.cloned.1.call-start = ((), (), s32[]{:S(2)}) async-start(), calls=%async_computation.16 | async-start | bytes 1327104 | tf_op jit(solution)/shard_map/all_gather | solution.py:102
  411.9 175.4 %all-gather.11.cloned.1.call-start = ((), (), s32[]{:S(2)}) async-start(), calls=%async_computation.5 | async-start | bytes 2506752 | tf_op jit(solution)/shard_map/all_gather | solution.py:60
  412.5 264.9 %all-reduce.6.cloned.1.call-start = ((), (), s32[]{:S(2)}) async-start(), calls=%async_computation.9 | async-start | bytes 2359296 | tf_op jit(solution)/shard_map/psum | solution.py:92
  466.7 93.9 %copy-start.6 = (f32[48,768]{1,0:T(8,128)}, f32[48,768]{1,0:T(8,128)S(1)}, u32[]{:S(2)}) copy-start(f32[48,768]{1,0:T(8,128)S(1)} %multiply_add_fusion.1) | copy-start | bytes 442372
  466.7 93.9 %copy-start.5 = (bf16[192,384]{1,0:T(8,128)(2,1)S(1)}, bf16[192,384]{1,0:T(8,128)(2,1)}, u32[]{:S(2)}) copy-start(bf16[192,384]{1,0:T(8,128)(2,1)} %convolution_convert_fusion.5) | copy-start | bytes 442372
  560.6 195.2 %reduce-scatter.11.cloned.1.call-start = ((), (), s32[]{:S(2)}) async-start(), calls=%async_computation.17 | async-start | bytes 2506752 | tf_op jit(solution)/shard_map/reduce_scatter | solution.py:103
  564.6 224.3 %reduce-scatter.5.cloned.1.call-start = ((), (), s32[]{:S(2)}) async-start(), calls=%async_computation.6 | async-start | bytes 663552 | tf_op jit(solution)/shard_map/reduce_scatter | solution.py:70
  587.3 27.3 %copy-start.1 = (bf16[3072,384]{1,0:T(8,128)(2,1)S(1)}, bf16[3072,384]{1,0:T(8,128)(2,1)}, u32[]{:S(2)}) copy-start(bf16[3072,384]{1,0:T(8,128)(2,1)} %all-gather.11.cloned.1.call-done) | copy-start | bytes 7077892
  617.3 260.7 %all-reduce.8.cloned.1.call-start = ((), (), s32[]{:S(2)}) async-start(), calls=%async_computation.10 | async-start | bytes 2359296 | tf_op jit(solution)/shard_map/psum | solution.py:92
  679.4 246.3 %copy-start.3 = (bf16[192,3072]{1,0:T(8,128)(2,1)S(1)}, bf16[192,3072]{1,0:T(8,128)(2,1)}, u32[]{:S(2)}) copy-start(bf16[192,3072]{1,0:T(8,128)(2,1)} %all-gather.21.cloned.1.call-done) | copy-start | bytes 3538948
  682.5 243.1 %all-gather.23.cloned.1.call-start = ((), (), s32[]{:S(2)}) async-start(), calls=%async_computation.18 | async-start | bytes 2506752 | tf_op jit(solution)/shard_map/all_gather | solution.py:114
  (4 other events, 50.4 us)
Sparse Core Ops, SparseCore 0:
  24.2 77.5 reduce-scatter.6
  104.0 24.8 all-gather.12
  131.6 54.4 all-gather.14
  260.0 20.8 all-gather.16
  284.7 75.7 reduce-scatter.8
  363.1 45.5 all-gather.18
  411.6 54.1 all-reduce.3
  468.0 45.9 all-gather.8
  516.2 22.8 all-gather.20
  541.6 45.6 all-gather.10
  590.6 86.8 all-reduce.5
  680.6 75.1 reduce-scatter.10
  758.2 30.7 reduce-scatter.4
  792.1 85.8 all-reduce.7
  880.6 45.0 all-gather.22
where the time goes:
time: 936 us; the launch traced here: 935 us
  waiting for transfers between devices  684 us (73%)
  blocking collectives  179 us (19%)
  matrix products  46.3 us (5%)
  between operations  15.6 us (2%)
    reduce_scatter x2, waiting for transfers between devices, local(): lax.psum_scatter(jnp.dot(iterate_rows.T, rounded_iterate, preferred_eleme...  149 us
    psum x2, waiting for transfers between devices, local(): lax.psum(partial_gram.astype(jnp.bfloat16), 'shard').astype(jnp.float32)  148 us
    reduce_scatter x1, waiting for transfers between devices, local(): lax.psum_scatter(jnp.dot(grad_rows.T, gradient, preferred_element_type=jn...  77.6 us
    all_gather x2, waiting for transfers between devices, local(): lax.all_gather(mixing, 'shard', axis=0, tiled=True)  66 us
    psum x1, blocking collectives, local(): total_right = lax.psum(local_right, ('shard', 'tensor'))  64.5 us
    all_gather x1, waiting for transfers between devices, local(): lax.all_gather(right_q, 'shard', axis=0, tiled=True)  57.2 us
    psum x1, waiting for transfers between devices, local(): lax.psum(left_terms.astype(jnp.bfloat16), 'tensor').astype(jnp.float32)  53.3 us
    all_gather x1, waiting for transfers between devices, local(): basis_all = lax.all_gather(basis_left, 'shard', axis=0, tiled=True)  47.2 us
  transfers between devices with their start and end apart: 15, of which 14 were waited for; matrix products, arithmetic and copies ran while one was open for 4% of the time, Pallas kernels for 0%

commit v1 on v0

--- a/solution.py
+++ b/solution.py
@@ -37,7 +37,9 @@
     row_start = shard_pos * rows_left
     grad_cols = lax.all_gather(gradient, "shard", axis=0, tiled=True)
     left_terms = jnp.dot(gradient, grad_cols.T, preferred_element_type=jnp.float32)
-    gram_rows = lax.psum(left_terms.astype(jnp.bfloat16), "tensor").astype(jnp.float32)
+    gram_rows = jnp.sum(lax.all_gather(left_terms.astype(jnp.bfloat16), "tensor"), axis=0).astype(
+        jnp.float32
+    )
     new_stat_left = blend_stat(stat_left, gram_rows, FF)
     grad_rows = lax.all_gather(gradient, "tensor", axis=1, tiled=True)
     gram_block = lax.psum_scatter(

time: 936 us -> 878 us (0.938)
  waiting for transfers between devices: 684 us -> 613 us
  blocking collectives: 179 us -> 193 us
    psum x1 -> x0, waiting for transfers between devices: 53.3 us -> none  [local(): lax.psum(left_terms.astype(jnp.bfloat16), 'tensor').astype(jnp.float32)]
    all_gather x1, waiting for transfers between devices: 47.2 us -> 5.34 us  [local(): basis_all = lax.all_gather(basis_left, 'shard', axis=0, tiled=True)]
    all_gather x2, waiting for transfers between devices: 66 us -> 89.9 us  [local(): lax.all_gather(mixing, 'shard', axis=0, tiled=True)]
    all_gather x0 -> x1, blocking collectives: none -> 13.5 us  [local(): lax.all_gather(left_terms.astype(jnp.bfloat16), 'tensor')]
  transfers between devices with their start and end apart: 15 -> 14, of which waited for: 14 -> 13; matrix products, arithmetic and copies ran while one was open for 4% -> 4% of each run, Pallas kernels for 0% -> 0%
where the time goes in v1:
time: 878 us; the launch traced here: 877 us
  waiting for transfers between devices  613 us (70%)
  blocking collectives  193 us (22%)
  matrix products  45.7 us (5%)
  between operations  15.6 us (2%)
    reduce_scatter x2, waiting for transfers between devices, local(): lax.psum_scatter(jnp.dot(iterate_rows.T, rounded_iterate, preferred_eleme...  149 us
    psum x2, waiting for transfers between devices, local(): lax.psum(partial_gram.astype(jnp.bfloat16), 'shard').astype(jnp.float32)  148 us
    all_gather x2, waiting for transfers between devices, local(): lax.all_gather(mixing, 'shard', axis=0, tiled=True)  89.9 us
    reduce_scatter x1, waiting for transfers between devices, local(): lax.psum_scatter(jnp.dot(grad_rows.T, gradient, preferred_element_type=jn...  77.5 us
    psum x1, blocking collectives, local(): total_right = lax.psum(local_right, ('shard', 'tensor'))  64.5 us
    all_gather x1, waiting for transfers between devices, local(): lax.all_gather(right_q, 'shard', axis=0, tiled=True)  57.2 us
    psum x1, blocking collectives, local(): total_left = lax.psum(local_left, 'shard')  39.1 us
    reduce_scatter x1, waiting for transfers between devices, local(): lax.psum_scatter(back_terms, 'tensor', scatter_dimension=1, tiled=True)  31.3 us
  transfers between devices with their start and end apart: 14, of which 13 were waited for; matrix products, arithmetic and copies ran while one was open for 4% of the time, Pallas kernels for 0%

profile of v1, /device:TPU:0, one launch (start us, length us, event | category | flops | bytes accessed | tf_op | source)
XLA Modules:
  0.0 877.2 jit_solution(11943040214229783819)
XLA Ops:
  7.2 13.8 %all_gather.49 = bf16[48,3072]{1,0:T(8,128)(2,1)S(1)} all-gather(bf16[48,384]{1,0:T(8,128)(2,1)} %param.7), channel_id=1, replica_groups=mesh['shard'=16,'tensor'=8] {'tensor'}, dimensions={1}, use_global_device_ids=true | all-gather | bytes 331776 | tf_op jit(solution)/shard_map/all_gather | solution.py:44
  24.2 77.5 %reduce-scatter.7.cloned.1.call-done = bf16[192,384]{1,0:T(8,128)(2,1)} async-done(((bf16[3072,384]{1,0:T(8,128)(2,1)}), bf16[192,384]{1,0:T(8,128)(2,1)}) %reduce-scatter.7.cloned.1.call-update) | async-done | bytes 147472 | tf_op jit(solution)/shard_map/reduce_scatter | solution.py:45
  104.3 24.5 %all-gather.14.cloned.1.call-done = f32[192,3072]{1,0:T(8,128)} async-done(((f32[192,384]{1,0:T(8,128)}), f32[192,3072]{1,0:T(8,128)}) %all-gather.14.cloned.1.call-update) | async-done | bytes 2359312 | tf_op jit(solution)/shard_map/all_gather | solution.py:75
  128.8 57.2 %all-gather.16.cloned.1.call-done = f32[3072,384]{1,0:T(8,128)} async-done(((f32[192,384]{1,0:T(8,128)}), f32[3072,384]{1,0:T(8,128)}) %all-gather.16.cloned.1.call-update) | async-done | bytes 4718608 | tf_op jit(solution)/shard_map/all_gather | solution.py:78
  185.9 7.8 multiply_reduce_fusion
  193.7 64.5 %psum.31 = f32[]{:T(128)} all-reduce(f32[]{:T(128)} %get-tuple-element.14), channel_id=1, replica_groups=mesh['shard'=16,'tensor'=8] {'shard','tensor'}, use_global_device_ids=true, to_apply=%region_8.0 | all-reduce | flops 1 | bytes 8 | tf_op jit(solution)/shard_map/psum | solution.py:88
  259.8 21.0 %all-gather.18.cloned.1.call-done = bf16[192,3072]{1,0:T(8,128)(2,1)} async-done(((bf16[192,384]{1,0:T(8,128)(2,1)}), bf16[192,3072]{1,0:T(8,128)(2,1)}) %all-gather.18.cloned.1.call-update) | async-done | bytes 1179664 | tf_op jit(solution)/shard_map/all_gather | solution.py:104
  280.7 3.8 convolution_convert_fusion.1
  284.6 75.8 %reduce-scatter.9.cloned.1.call-done = bf16[192,384]{1,0:T(8,128)(2,1)} async-done(((bf16[3072,384]{1,0:T(8,128)(2,1)}), bf16[192,384]{1,0:T(8,128)(2,1)}) %reduce-scatter.9.cloned.1.call-update) | async-done | bytes 147472 | tf_op jit(solution)/shard_map/reduce_scatter | solution.py:105
  362.9 44.9 %all-gather.20.cloned.1.call-done = bf16[3072,384]{1,0:T(8,128)(2,1)} async-done(((bf16[192,384]{1,0:T(8,128)(2,1)}), bf16[3072,384]{1,0:T(8,128)(2,1)}) %all-gather.20.cloned.1.call-update) | async-done | bytes 2359312 | tf_op jit(solution)/shard_map/all_gather | solution.py:116
  411.8 24.2 %all_gather.43 = bf16[768,384]{1,0:T(8,128)(2,1)S(1)} all-gather(bf16[48,384]{1,0:T(8,128)(2,1)S(1)} %copy-done.7), channel_id=1, replica_groups=mesh['shard'=16,'tensor'=8] {'shard'}, dimensions={0}, use_global_device_ids=true | all-gather | bytes 626688 | tf_op jit(solution)/shard_map/all_gather | solution.py:38
  436.3 13.5 %all-gather = bf16[384,768]{1,0:T(8,128)(2,1)S(1)} all-gather(bf16[48,768]{1,0:T(8,128)(2,1)S(1)} %convolution_convert_fusion.6), channel_id=2, replica_groups=mesh['shard'=16,'tensor'=8] {'tensor'}, dimensions={0}, use_global_device_ids=true | all-gather | bytes 663552 | tf_op jit(solution)/shard_map/all_gather | solution.py:40
  450.0 5.3 all-gather.10.cloned.1.call-done
  455.3 3.8 multiply_reduce_fusion.1
  459.2 39.1 %psum.28 = f32[]{:T(128)} all-reduce(f32[]{:T(128)} %get-tuple-element.12), channel_id=1, replica_groups=mesh['shard'=16,'tensor'=8] {'shard'}, use_global_device_ids=true, to_apply=%region_4.0 | all-reduce | flops 1 | bytes 8 | tf_op jit(solution)/shard_map/psum | solution.py:87
  502.2 3.9 convolution_convert_fusion
  507.4 13.3 %all_gather.44 = bf16[48,3072]{1,0:T(8,128)(2,1)S(1)} all-gather(bf16[48,384]{1,0:T(8,128)(2,1)S(1)} %convolution_convert_fusion.8), channel_id=1, replica_groups=mesh['shard'=16,'tensor'=8] {'tensor'}, dimensions={1}, use_global_device_ids=true | all-gather | bytes 331776 | tf_op jit(solution)/shard_map/all_gather | solution.py:63
  520.7 8.1 all-gather.12.cloned.1.call-done
  531.8 24.5 %all_gather.46 = bf16[768,384]{1,0:T(8,128)(2,1)S(1)} all-gather(bf16[48,384]{1,0:T(8,128)(2,1)S(1)} %get-tuple-element.7), channel_id=1, replica_groups=mesh['shard'=16,'tensor'=8] {'shard'}, dimensions={0}, use_global_device_ids=true | all-gather | bytes 626688 | tf_op jit(solution)/shard_map/all_gather | solution.py:68
  559.1 59.9 %all-reduce.3.cloned.1.call-done = bf16[768,768]{1,0:T(8,128)(2,1)} async-done(((bf16[768,768]{1,0:T(8,128)(2,1)}), bf16[768,768]{1,0:T(8,128)(2,1)}) %all-reduce.3.cloned.1.call-update) | async-done | bytes 1179664 | tf_op jit(solution)/shard_map/psum | solution.py:94
  624.1 73.4 %reduce-scatter.11.cloned.1.call-done = bf16[192,384]{1,0:T(8,128)(2,1)} async-done(((bf16[3072,384]{1,0:T(8,128)(2,1)}), bf16[192,384]{1,0:T(8,128)(2,1)}) %reduce-scatter.11.cloned.1.call-update) | async-done | bytes 147472 | tf_op jit(solution)/shard_map/reduce_scatter | solution.py:105
  699.2 31.3 %reduce-scatter.5.cloned.1.call-done = f32[48,384]{1,0:T(8,128)} async-done(((f32[48,3072]{1,0:T(8,128)}), f32[48,384]{1,0:T(8,128)}) %reduce-scatter.5.cloned.1.call-update) | async-done | bytes 73744 | tf_op jit(solution)/shard_map/reduce_scatter | solution.py:72
  732.0 87.8 %all-reduce.5.cloned.1.call-done = bf16[768,768]{1,0:T(8,128)(2,1)} async-done(((bf16[768,768]{1,0:T(8,128)(2,1)}), bf16[768,768]{1,0:T(8,128)(2,1)}) %all-reduce.5.cloned.1.call-update) | async-done | bytes 1179664 | tf_op jit(solution)/shard_map/psum | solution.py:94
  822.5 45.0 %all-gather.24.cloned.1.call-done = bf16[3072,384]{1,0:T(8,128)(2,1)} async-done(((bf16[192,384]{1,0:T(8,128)(2,1)}), bf16[3072,384]{1,0:T(8,128)(2,1)}) %all-gather.24.cloned.1.call-update) | async-done | bytes 2359312 | tf_op jit(solution)/shard_map/all_gather | solution.py:116
  (77 shorter events, 37.7 us)
Async XLA Ops:
  7.2 94.5 %reduce-scatter.7.cloned.1.call-start = ((), (), s32[]{:S(2)}) async-start(), calls=%async_computation.7 | async-start | bytes 2506752 | tf_op jit(solution)/shard_map/reduce_scatter | solution.py:45
  21.0 80.7 %copy-start.8 = (f32[192,384]{1,0:T(8,128)S(1)}, f32[192,384]{1,0:T(8,128)}, u32[]{:S(2)}) copy-start(f32[192,384]{1,0:T(8,128)} %param.11) | copy-start | bytes 884740
  24.1 79.3 %copy-start.9 = (f32[192,384]{1,0:T(8,128)S(1)}, f32[192,384]{1,0:T(8,128)}, u32[]{:S(2)}) copy-start(f32[192,384]{1,0:T(8,128)} %param.13) | copy-start | bytes 884740
  24.1 104.7 %all-gather.14.cloned.1.call-start = ((), (), s32[]{:S(2)}) async-start(), calls=%async_computation.10 | async-start | bytes 2654208 | tf_op jit(solution)/shard_map/all_gather | solution.py:75
  103.3 82.6 %all-gather.16.cloned.1.call-start = ((), (), s32[]{:S(2)}) async-start(), calls=%async_computation.11 | async-start | bytes 5013504 | tf_op jit(solution)/shard_map/all_gather | solution.py:78
  104.2 176.5 %all-gather.18.cloned.1.call-start = ((), (), s32[]{:S(2)}) async-start(), calls=%async_computation.12 | async-start | bytes 1327104 | tf_op jit(solution)/shard_map/all_gather | solution.py:104
  259.7 100.7 %reduce-scatter.9.cloned.1.call-start = ((), (), s32[]{:S(2)}) async-start(), calls=%async_computation.13 | async-start | bytes 2506752 | tf_op jit(solution)/shard_map/reduce_scatter | solution.py:105
  284.5 123.4 %copy-start.4 = (bf16[192,3072]{1,0:T(8,128)(2,1)S(1)}, bf16[192,3072]{1,0:T(8,128)(2,1)}, u32[]{:S(2)}) copy-start(bf16[192,3072]{1,0:T(8,128)(2,1)} %all-gather.18.cloned.1.call-done) | copy-start | bytes 3538948
  284.5 123.3 %all-gather.20.cloned.1.call-start = ((), (), s32[]{:S(2)}) async-start(), calls=%async_computation.14 | async-start | bytes 2506752 | tf_op jit(solution)/shard_map/all_gather | solution.py:116
  362.1 93.2 %all-gather.10.cloned.1.call-start = ((), (), s32[]{:S(2)}) async-start(), calls=%async_computation.4 | async-start | bytes 2506752 | tf_op jit(solution)/shard_map/all_gather | solution.py:52
  362.9 48.9 %copy-start.7 = (bf16[48,384]{1,0:T(8,128)(2,1)S(1)}, bf16[48,384]{1,0:T(8,128)(2,1)}, u32[]{:S(2)}) copy-start(bf16[48,384]{1,0:T(8,128)(2,1)} %param.7) | copy-start | bytes 110596
  362.9 139.3 %all-gather.22.cloned.1.call-start = ((), (), s32[]{:S(2)}) async-start(), calls=%async_computation.15 | async-start | bytes 1327104 | tf_op jit(solution)/shard_map/all_gather | solution.py:104
  410.9 39.0 %copy-start.10 = (f32[48,768]{1,0:T(8,128)S(1)}, f32[48,768]{1,0:T(8,128)}, u32[]{:S(2)}) copy-start(f32[48,768]{1,0:T(8,128)} %param.10) | copy-start | bytes 442372
  411.0 117.8 %all-gather.12.cloned.1.call-start = ((), (), s32[]{:S(2)}) async-start(), calls=%async_computation.5 | async-start | bytes 2506752 | tf_op jit(solution)/shard_map/all_gather | solution.py:62
  411.7 207.3 %all-reduce.3.cloned.1.call-start = ((), (), s32[]{:S(2)}) async-start(), calls=%async_computation.8 | async-start | bytes 2359296 | tf_op jit(solution)/shard_map/psum | solution.py:94
  450.0 52.1 %copy-start.6 = (f32[48,768]{1,0:T(8,128)}, f32[48,768]{1,0:T(8,128)S(1)}, u32[]{:S(2)}) copy-start(f32[48,768]{1,0:T(8,128)S(1)} %multiply_add_fusion.1) | copy-start | bytes 442372
  450.0 52.2 %copy-start.5 = (bf16[192,384]{1,0:T(8,128)(2,1)S(1)}, bf16[192,384]{1,0:T(8,128)(2,1)}, u32[]{:S(2)}) copy-start(bf16[192,384]{1,0:T(8,128)(2,1)} %convolution_convert_fusion.5) | copy-start | bytes 442372
  502.1 195.4 %reduce-scatter.11.cloned.1.call-start = ((), (), s32[]{:S(2)}) async-start(), calls=%async_computation.16 | async-start | bytes 2506752 | tf_op jit(solution)/shard_map/reduce_scatter | solution.py:105
  506.1 22.7 %copy-start.11 = (f32[48,384]{1,0:T(8,128)S(1)}, f32[48,384]{1,0:T(8,128)}, u32[]{:S(2)}) copy-start(f32[48,384]{1,0:T(8,128)} %param.8) | copy-start | bytes 221188
  506.1 224.4 %reduce-scatter.5.cloned.1.call-start = ((), (), s32[]{:S(2)}) async-start(), calls=%async_computation.6 | async-start | bytes 663552 | tf_op jit(solution)/shard_map/reduce_scatter | solution.py:72
  528.8 27.5 %copy-start.1 = (bf16[3072,384]{1,0:T(8,128)(2,1)S(1)}, bf16[3072,384]{1,0:T(8,128)(2,1)}, u32[]{:S(2)}) copy-start(bf16[3072,384]{1,0:T(8,128)(2,1)} %all-gather.12.cloned.1.call-done) | copy-start | bytes 7077892
  559.0 260.8 %all-reduce.5.cloned.1.call-start = ((), (), s32[]{:S(2)}) async-start(), calls=%async_computation.9 | async-start | bytes 2359296 | tf_op jit(solution)/shard_map/psum | solution.py:94
  621.0 246.5 %copy-start.3 = (bf16[192,3072]{1,0:T(8,128)(2,1)S(1)}, bf16[192,3072]{1,0:T(8,128)(2,1)}, u32[]{:S(2)}) copy-start(bf16[192,3072]{1,0:T(8,128)(2,1)} %all-gather.22.cloned.1.call-done) | copy-start | bytes 3538948
  624.1 243.4 %all-gather.24.cloned.1.call-start = ((), (), s32[]{:S(2)}) async-start(), calls=%async_computation.17 | async-start | bytes 2506752 | tf_op jit(solution)/shard_map/all_gather | solution.py:116
  (3 other events, 27.8 us)
Sparse Core Ops, SparseCore 0:
  24.2 77.3 reduce-scatter.6
  103.9 24.8 all-gather.13
  131.5 54.4 all-gather.15
  259.8 20.8 all-gather.17
  284.6 75.7 reduce-scatter.8
  363.0 44.8 all-gather.19
  410.0 45.2 all-gather.9
  457.6 22.8 all-gather.21
  483.2 45.6 all-gather.11
  531.9 86.9 all-reduce.2
  622.3 75.1 reduce-scatter.10
  699.7 30.7 reduce-scatter.4
  733.8 85.9 all-reduce.4
  822.4 45.0 all-gather.23
